TPU v7x, 32 devices: a whole 2x2x4 slice. The times are simulated.
32 devices in a mesh: grp: 4 (over z), blk: 8 (over y, x, core).
Axes of the slice: x: 2, y: 2, z: 4, core: 2. Of those that a mesh axis runs over, the one named last changes fastest.
Arguments:
- tokens: bfloat16 [8192, 2048], P(('grp', 'blk')), may hold values from -9 to 9
- block_group: int32 [64], replicated, may hold values from 0 to 3, as said below
- block_slot: int32 [64], replicated, may hold values from 0 to 15, as said below
- attn_gain: bfloat16 [2048], P(('grp', 'blk')), may hold values from 0.5 to 1.5
- w_query: bfloat16 [2048, 2048], P(('grp', 'blk')), may hold values from -0.5 to 0.5
- w_key: bfloat16 [2048, 512], P(('grp', 'blk')), may hold values from -0.5 to 0.5
- w_value: bfloat16 [2048, 512], P(('grp', 'blk')), may hold values from -0.125 to 0.125
- w_out: bfloat16 [2048, 2048], P(('grp', 'blk')), may hold values from -2 to 2
- mlp_gain: bfloat16 [2048], P(('grp', 'blk')), may hold values from 0.5 to 1.5
- w_gate: bfloat16 [2048, 8192], P(None, ('grp', 'blk')), may hold values from -0.125 to 0.125
- w_up: bfloat16 [2048, 8192], P(None, ('grp', 'blk')), may hold values from -0.125 to 0.125
- w_down: bfloat16 [8192, 2048], P(('grp', 'blk')), may hold values from -0.5 to 0.5
- cotangent: bfloat16 [8192, 2048], P(('grp', 'blk')), may hold values from -6 to 6
Outputs:
- output: bfloat16 [8192, 2048], P(('grp', 'blk'))
- tokens_grad: bfloat16 [8192, 2048], P(('grp', 'blk'))
- attn_gain_grad: float32 [2048], P(('grp', 'blk'))
- w_query_grad: float32 [2048, 2048], P(('grp', 'blk'))
- w_key_grad: float32 [2048, 512], P(('grp', 'blk'))
- w_value_grad: float32 [2048, 512], P(('grp', 'blk'))
- w_out_grad: float32 [2048, 2048], P(('grp', 'blk'))
- mlp_gain_grad: float32 [2048], P(('grp', 'blk'))
- w_gate_grad: float32 [2048, 8192], P(None, ('grp', 'blk'))
- w_up_grad: float32 [2048, 8192], P(None, ('grp', 'blk'))
- w_down_grad: float32 [8192, 2048], P(('grp', 'blk'))
- rms_stats: float32 [3], replicated
Inputs may be any that keep to these rules, and one draw needn't show every extreme that they name: `block_group`: each group has 16 blocks, one of each slot, and all of them lie in one aligned run of 16 blocks. `block_slot`: slots below 8 are the prompt's parts in order, the others its continuations.
All inputs are finite; a program needn't handle non-finite values.
Results may differ from a plain program's by a relative error of at most 0.019.
Values may be sent and summed in bfloat16 or wider, within the bound.
A program may use at most 448 MiB of HBM per device.

v0:
```python
import jax
import jax.numpy as jnp
from jax import lax
from jax.sharding import Mesh
from jax.sharding import PartitionSpec as P

D = 2048
HEADS = 32
KV_HEADS = 8
HEAD_DIM = 64
BLOCK = 128
PROMPT_BLOCKS = 8
GROUP_BLOCKS = 16
PER_GROUP = HEADS // KV_HEADS
ATTN_MULT = 0.015625
RESID_MULT = 0.22
EPSILON = 1e-05
MASKED = -1e30
PLANE = ("chip", "core")
EVERY = ("grp", "chip", "core")
BF16 = jnp.bfloat16
F32 = jnp.float32


def matmul(left, right):
    return jnp.dot(left, right, preferred_element_type=F32)


def over_rows(left, right):
    return lax.dot_general(left, right, (((0,), (0,)), ((), ())), preferred_element_type=F32)


def over_cols(left, right):
    return lax.dot_general(left, right, (((1,), (1,)), ((), ())), preferred_element_type=F32)


def gather(values, axes, axis=0):
    return lax.all_gather(values, axes, axis=axis, tiled=True)


def scatter(values, axes, axis=0):
    return lax.psum_scatter(values, axes, scatter_dimension=axis, tiled=True)


def norm_parts(values):
    factor = lax.rsqrt(jnp.mean(values * values, axis=-1, keepdims=True) + EPSILON)
    return factor


def norm_back(values, factor, gain, grad):
    scaled = gain * grad
    inner = jnp.mean(values * scaled, axis=-1, keepdims=True)
    return (
        factor * scaled - values * (factor * factor * factor * inner),
        jnp.sum(grad * values * factor, axis=0),
    )


def on_device(
    tokens,
    block_group,
    block_slot,
    attn_gain,
    w_query,
    w_key,
    w_value,
    w_out,
    mlp_gain,
    w_gate,
    w_up,
    w_down,
    cotangent,
):
    tok_axes, weight_axes = (TOK_AXES, WEIGHT_AXES)
    grps = lax.axis_size("grp")
    devs = lax.axis_size(PLANE)
    rows = tokens.shape[0]
    w_rows = w_query.shape[0]
    q_heads = HEADS // devs
    kv_heads = max(1, KV_HEADS // devs)
    kv_copies = max(1, devs // KV_HEADS)
    q_cols, kv_cols = (q_heads * HEAD_DIM, kv_heads * HEAD_DIM)
    row_blocks = rows // BLOCK * devs
    row_groups = row_blocks // GROUP_BLOCKS
    row_first = lax.axis_index("grp") * row_blocks
    keys = lax.dynamic_slice_in_dim(block_group, row_first, row_blocks) * GROUP_BLOCKS
    keys = keys + lax.dynamic_slice_in_dim(block_slot, row_first, row_blocks)
    rank = jnp.sum((keys[None, :] < keys[:, None]).astype(jnp.int32), axis=1)
    ids = jnp.arange(row_blocks, dtype=jnp.int32)
    order = jnp.sum(jnp.where(rank[None, :] == ids[:, None], ids[None, :], 0), axis=1)

    def kv_split(w):
        w = w.reshape(w_rows, devs // kv_copies, kv_cols)
        return jnp.repeat(w, kv_copies, axis=1) if kv_copies > 1 else w

    gains = jnp.stack([attn_gain, mlp_gain], axis=1)
    gains = jnp.broadcast_to(jnp.pad(gains, ((0, 0), (0, 126)))[:, None, :], (w_rows, devs, 128))
    packed = jnp.concatenate(
        [w_query.reshape(w_rows, devs, q_cols), kv_split(w_key), kv_split(w_value), gains], axis=2
    )
    packed = lax.all_to_all(packed, PLANE, split_axis=1, concat_axis=0, tiled=True)
    packed = gather(packed.reshape(devs * w_rows, q_cols + 2 * kv_cols + 128), "grp")
    w_qkv = packed[:, : q_cols + 2 * kv_cols]
    gain_one = packed[:, q_cols + 2 * kv_cols].astype(F32)
    gain_two = packed[:, q_cols + 2 * kv_cols + 1].astype(F32)
    all_tokens = gather(tokens, PLANE)
    layer_all = all_tokens.astype(F32)
    normed_one = (layer_all * norm_parts(layer_all) * gain_one).astype(BF16)
    qkv = matmul(normed_one, w_qkv).astype(BF16)
    qkv = qkv.reshape(row_blocks, BLOCK, q_cols + 2 * kv_cols)[order]
    qkv = qkv.reshape(row_groups, GROUP_BLOCKS * BLOCK, q_cols + 2 * kv_cols)
    seq = GROUP_BLOCKS * BLOCK
    per_kv = q_heads // kv_heads
    q = qkv[:, :, :q_cols].reshape(row_groups, seq, kv_heads, per_kv, HEAD_DIM)
    k = qkv[:, :, q_cols : q_cols + kv_cols].reshape(row_groups, seq, kv_heads, HEAD_DIM)
    v = qkv[:, :, q_cols + kv_cols :].reshape(row_groups, seq, kv_heads, HEAD_DIM)
    prompt = PROMPT_BLOCKS * BLOCK
    row_id = jnp.arange(seq)
    q_b = q.reshape(row_groups, GROUP_BLOCKS, BLOCK, kv_heads, per_kv, HEAD_DIM)
    k_b = k.reshape(row_groups, GROUP_BLOCKS, BLOCK, kv_heads, HEAD_DIM)
    v_b = v.reshape(row_groups, GROUP_BLOCKS, BLOCK, kv_heads, HEAD_DIM)
    k_p, v_p = (k[:, :prompt], v[:, :prompt])
    starts = jnp.minimum(jnp.arange(GROUP_BLOCKS), PROMPT_BLOCKS) * BLOCK
    see_p = jnp.arange(prompt)[None, :] < starts[:, None]
    see_o = jnp.arange(BLOCK)[None, :] <= jnp.arange(BLOCK)[:, None]

    def all_scores():
        far = jnp.einsum("gbikpd,gjkd->gbkpij", q_b, k_p, preferred_element_type=F32)
        far = jnp.where(see_p[None, :, None, None, None, :], far * ATTN_MULT, MASKED)
        own = jnp.einsum("gbikpd,gbjkd->gbkpij", q_b, k_b, preferred_element_type=F32)
        own = jnp.where(see_o[None, None, None, None, :, :], own * ATTN_MULT, MASKED)
        return (far, own)

    far, own = all_scores()
    peak = jnp.maximum(far.max(-1, keepdims=True), own.max(-1, keepdims=True))
    far, own = (jnp.exp(far - peak), jnp.exp(own - peak))
    total = far.sum(-1, keepdims=True) + own.sum(-1, keepdims=True)
    far_p, own_p = (far / total, own / total)
    attended = jnp.einsum(
        "gbkpij,gjkd->gbikpd", far_p.astype(BF16), v_p, preferred_element_type=F32
    ) + jnp.einsum("gbkpij,gbjkd->gbikpd", own_p.astype(BF16), v_b, preferred_element_type=F32)
    attended = attended.astype(BF16).reshape(row_blocks, BLOCK, q_cols)[rank]
    attended = lax.all_to_all(
        attended.reshape(row_blocks * BLOCK, q_cols), PLANE, split_axis=0, concat_axis=1, tiled=True
    )
    out_full = gather(w_out, EVERY)
    layer_in = tokens.astype(F32)
    branch_attn = matmul(attended, out_full)
    residual = layer_in + RESID_MULT * branch_attn
    factor_two = norm_parts(residual)
    normed_two = gather((residual * factor_two * gain_two).astype(BF16), tok_axes)
    upstream = cotangent.astype(F32)
    d_branch_mlp = gather((RESID_MULT * upstream).astype(BF16), tok_axes)
    gate_w = gather(w_gate, weight_axes, axis=1)
    up_w = gather(w_up, weight_axes, axis=1)
    down_w = gather(w_down, weight_axes)
    gate_act = matmul(normed_two, gate_w)
    up_act = matmul(normed_two, up_w)
    sig = jax.nn.sigmoid(gate_act)
    silu = gate_act * sig
    hidden = (silu * up_act).astype(BF16)
    branch_mlp = scatter(matmul(hidden, down_w).astype(BF16), tok_axes).astype(F32)
    layer_out = residual + RESID_MULT * branch_mlp
    grad_down = scatter(over_rows(hidden, d_branch_mlp).astype(BF16), weight_axes).astype(F32)
    d_hidden = over_cols(d_branch_mlp, down_w)
    d_gate = (d_hidden * up_act * (sig * (1.0 + gate_act * (1.0 - sig)))).astype(BF16)
    d_up = (d_hidden * silu).astype(BF16)
    grad_gate = scatter(over_rows(normed_two, d_gate).astype(BF16), weight_axes, axis=1).astype(F32)
    grad_up = scatter(over_rows(normed_two, d_up).astype(BF16), weight_axes, axis=1).astype(F32)
    d_normed_two = over_cols(d_gate, gate_w) + over_cols(d_up, up_w)
    d_normed_two = scatter(d_normed_two.astype(BF16), tok_axes).astype(F32)
    d_residual_norm, d_gain_two = norm_back(residual, factor_two, gain_two, d_normed_two)
    d_residual = upstream + d_residual_norm
    d_branch_attn = (RESID_MULT * d_residual).astype(BF16)
    grad_out = scatter(over_rows(attended, d_branch_attn).astype(BF16), EVERY).astype(F32)
    d_attended = over_cols(d_branch_attn, out_full).astype(BF16)
    d_attended = lax.all_to_all(d_attended, PLANE, split_axis=1, concat_axis=0, tiled=True)
    d_b = d_attended.reshape(row_blocks, BLOCK, q_cols)[order]
    d_b = d_b.reshape(row_groups, GROUP_BLOCKS, BLOCK, kv_heads, per_kv, HEAD_DIM)
    far_s = jnp.einsum("gbikpd,gjkd->gbkpij", d_b, v_p, preferred_element_type=F32)
    own_s = jnp.einsum("gbikpd,gbjkd->gbkpij", d_b, v_b, preferred_element_type=F32)
    mean_s = (far_p * far_s).sum(-1, keepdims=True) + (own_p * own_s).sum(-1, keepdims=True)
    far_d = (far_p * (far_s - mean_s)).astype(BF16)
    own_d = (own_p * (own_s - mean_s)).astype(BF16)
    far_p, own_p = (far_p.astype(BF16), own_p.astype(BF16))
    d_q = ATTN_MULT * (
        jnp.einsum("gbkpij,gjkd->gbikpd", far_d, k_p, preferred_element_type=F32)
        + jnp.einsum("gbkpij,gbjkd->gbikpd", own_d, k_b, preferred_element_type=F32)
    )
    d_k = jnp.einsum("gbkpij,gbikpd->gbjkd", own_d, q_b, preferred_element_type=F32)
    d_v = jnp.einsum("gbkpij,gbikpd->gbjkd", own_p, d_b, preferred_element_type=F32)
    d_kp = jnp.einsum("gbkpij,gbikpd->gjkd", far_d, q_b, preferred_element_type=F32)
    d_vp = jnp.einsum("gbkpij,gbikpd->gjkd", far_p, d_b, preferred_element_type=F32)
    d_k = ATTN_MULT * jnp.concatenate(
        [
            d_k.reshape(row_groups, seq, kv_cols)[:, :prompt]
            + d_kp.reshape(row_groups, prompt, kv_cols),
            d_k.reshape(row_groups, seq, kv_cols)[:, prompt:],
        ],
        axis=1,
    )
    d_v = jnp.concatenate(
        [
            d_v.reshape(row_groups, seq, kv_cols)[:, :prompt]
            + d_vp.reshape(row_groups, prompt, kv_cols),
            d_v.reshape(row_groups, seq, kv_cols)[:, prompt:],
        ],
        axis=1,
    )
    d_qkv = jnp.concatenate([d_q.reshape(row_groups, seq, q_cols), d_k, d_v], axis=2).astype(BF16)
    d_qkv = d_qkv.reshape(row_blocks, BLOCK, q_cols + 2 * kv_cols)[rank]
    d_qkv = d_qkv.reshape(row_blocks * BLOCK, q_cols + 2 * kv_cols)
    d_normed_one = scatter(over_cols(d_qkv, w_qkv).astype(BF16), PLANE).astype(F32)
    d_input_norm, d_gain_one = norm_back(layer_in, norm_parts(layer_in), gain_one, d_normed_one)
    tokens_grad = (d_residual + d_input_norm).astype(BF16)
    grad_qkv = over_rows(normed_one, d_qkv)
    d_gains = jnp.pad(jnp.stack([d_gain_one, d_gain_two], axis=1), ((0, 0), (0, 126)))
    sent = scatter(jnp.concatenate([grad_qkv, d_gains], axis=1).astype(BF16), "grp")
    sent = sent.reshape(devs, w_rows, q_cols + 2 * kv_cols + 128)
    sent = lax.all_to_all(sent, PLANE, split_axis=0, concat_axis=0, tiled=True).astype(F32)

    def kv_join(g):
        g = g.reshape(devs // kv_copies, kv_copies, w_rows, kv_cols)
        g = jnp.sum(g, axis=1) if kv_copies > 1 else g[:, 0]
        return jnp.swapaxes(g, 0, 1).reshape(w_rows, KV_HEADS * HEAD_DIM)

    grad_query = jnp.swapaxes(sent[:, :, :q_cols], 0, 1).reshape(w_rows, D)
    grad_key = kv_join(sent[:, :, q_cols : q_cols + kv_cols])
    grad_value = kv_join(sent[:, :, q_cols + kv_cols : q_cols + 2 * kv_cols])
    gains_sum = jnp.sum(sent[:, :, q_cols + 2 * kv_cols :], axis=0)
    scaled_attn = RESID_MULT * branch_attn
    scaled_mlp = RESID_MULT * branch_mlp
    squares = jnp.stack(
        [
            jnp.sum(layer_out * layer_out),
            jnp.sum(scaled_attn * scaled_attn),
            jnp.sum(scaled_mlp * scaled_mlp),
        ]
    )
    totals = lax.psum(squares, EVERY)
    rms_stats = jnp.sqrt(totals / (rows * grps * devs * D))
    return (
        layer_out.astype(BF16),
        tokens_grad,
        gains_sum[:, 0],
        grad_query,
        grad_key,
        grad_value,
        grad_out,
        gains_sum[:, 1],
        grad_gate,
        grad_up,
        grad_down,
        rms_stats,
    )


TOK_AXES, WEIGHT_AXES = (PLANE, ("grp",))


def solution(mesh):
    shape = (mesh.shape["grp"], mesh.shape["blk"] // 2, 2)
    mesh = Mesh(mesh.devices.reshape(shape), EVERY)
    row, col, vec = (P(EVERY, None), P(None, EVERY), P(EVERY))
    return jax.shard_map(
        on_device,
        mesh=mesh,
        in_specs=(row, P(), P(), vec, row, row, row, row, vec, col, col, row, row),
        out_specs=(row, row, vec, row, row, row, row, vec, col, col, row, P()),
        check_vma=False,
    )
```

profile of v0, /device:TPU:0, one launch (start us, length us, event | category | flops | bytes accessed | tf_op | source)
XLA Modules:
  0.0 1417.4 jit_solution(8293760625746567301)
XLA Ops:
  11.4 14.8 %all_to_all.55 = bf16[64,8,512]{2,0,1:T(8,128)(2,1)} all-to-all(bf16[64,8,512]{2,0,1:T(8,128)(2,1)S(1)} %copy.186), channel_id=1, replica_groups=mesh['grp'=4,'chip'=4,'core'=2] {'chip','core'}, dimensions={1} | all-to-all | bytes 1048576 | tf_op jit(solution)/shard_map/all_to_all | solution.py:101
  28.9 42.7 %all-gather.11.cloned.1.call-done = bf16[2048,512]{1,0:T(8,128)(2,1)} async-done(((bf16[512,512]{1,0:T(8,128)(2,1)}), bf16[2048,512]{1,0:T(8,128)(2,1)}) %all-gather.11.cloned.1.call-update) | async-done | bytes 2097168 | tf_op jit(solution)/shard_map/all_gather | solution.py:38
  71.7 1.8 convert_reduce_fusion
  73.5 53.2 %all-gather.9.cloned.1.call-done = bf16[2048,2048]{1,0:T(8,128)(2,1)} async-done(((bf16[256,2048]{1,0:T(8,128)(2,1)}), bf16[2048,2048]{1,0:T(8,128)(2,1)}) %all-gather.9.cloned.1.call-update) | async-done | bytes 8388624 | tf_op jit(solution)/shard_map/all_gather | solution.py:38
  126.7 5.2 fusion.6
  132.5 6.2 convolution_convert_fusion.7
  142.9 3.5 reshape.454
  147.5 4.0 fusion.21
  151.5 5.3 fusion.5
  156.8 6.5 fusion.20
  163.3 9.2 fusion.4
  173.9 15.7 %fusion.42 = bf16[1,16,128,1,4,64]{2,5,4,1,3,0:T(8,128)(2,1)S(1)} fusion(f32[16,64,4,128]{3,1,2,0:T(8,128)S(1)} %fusion.45, bf16[1,2048,1,64]{1,3,2,0:T(8,128)(2,1)S(1)} %bitcast.311, f32[16,4,128]{2,1,0:T(4,128)S(1)} %add.138, f32[16,4,128]{2,1,0:T(4,128)S(1)} %max.8, f32[1024,16,128,4]{2,0,3,1:T(8,128)} %copy-done, ...), kind=kOutput, calls=%fused_computation.82 | convolution fusion | flops 1116733440 | bytes 36913152 | tf_op jit(solution)/shard_map/gbkpij,gjkd->gbikpd/dot_general | solution.py:139
  190.8 18.6 %all_to_all.56 = bf16[8,256,256]{2,1,0:T(8,128)(2,1)S(1)} all-to-all(bf16[8,256,256]{2,1,0:T(8,128)(2,1)S(1)} %bitcast.291), channel_id=1, replica_groups=mesh['grp'=4,'chip'=4,'core'=2] {'chip','core'}, dimensions={0} | all-to-all | bytes 2097152 | tf_op jit(solution)/shard_map/all_to_all | solution.py:143
  209.4 1.3 copy.195
  210.7 7.5 multiply_reduce_fusion.3
  222.2 65.5 %all-gather.19.cloned.1.call-done = bf16[2048,1024]{1,0:T(8,128)(2,1)} async-done(((bf16[2048,256]{1,0:T(8,128)(2,1)}), bf16[2048,1024]{1,0:T(8,128)(2,1)}) %all-gather.19.cloned.1.call-update) | async-done | bytes 4194320 | tf_op jit(solution)/shard_map/all_gather | solution.py:38
  287.7 54.9 %all-gather.15.cloned.1.call-done = bf16[2048,2048]{1,0:T(8,128)(2,1)} async-done(((bf16[256,2048]{1,0:T(8,128)(2,1)}), bf16[2048,2048]{1,0:T(8,128)(2,1)}) %all-gather.15.cloned.1.call-update) | async-done | bytes 8388624 | tf_op jit(solution)/shard_map/all_gather | solution.py:38
  342.6 14.8 %fusion.94 = f32[2048,1024]{1,0:T(8,128)} fusion(bf16[2048,2048]{1,0:T(8,128)(2,1)} %all-gather.15.cloned.1.call-done, bf16[2048,1024]{1,0:T(8,128)(2,1)} %all-gather.19.cloned.1.call-done), kind=kOutput, calls=%fused_computation.166 | convolution fusion | flops 8589934592 | bytes 20971520 | tf_op jit(solution)/shard_map/dot_general | solution.py:26
  357.4 67.2 %all-gather.17.cloned.1.call-done = bf16[2048,1024]{1,0:T(8,128)(2,1)} async-done(((bf16[2048,256]{1,0:T(8,128)(2,1)}), bf16[2048,1024]{1,0:T(8,128)(2,1)}) %all-gather.17.cloned.1.call-update) | async-done | bytes 4194320 | tf_op jit(solution)/shard_map/all_gather | solution.py:38
  424.6 14.4 %fusion.93 = f32[2048,1024]{1,0:T(8,128)} fusion(bf16[2048,2048]{1,0:T(8,128)(2,1)} %all-gather.15.cloned.1.call-done, bf16[2048,1024]{1,0:T(8,128)(2,1)} %all-gather.17.cloned.1.call-done), kind=kOutput, calls=%fused_computation.165 | convolution fusion | flops 8589934592 | bytes 20971520 | tf_op jit(solution)/shard_map/dot_general | solution.py:26
  439.0 66.2 %all-gather.21.cloned.1.call-done = bf16[1024,2048]{1,0:T(8,128)(2,1)} async-done(((bf16[256,2048]{1,0:T(8,128)(2,1)}), bf16[1024,2048]{1,0:T(8,128)(2,1)}) %all-gather.21.cloned.1.call-update) | async-done | bytes 4194320 | tf_op jit(solution)/shard_map/all_gather | solution.py:38
  505.2 55.4 %all-gather.23.cloned.1.call-done = bf16[2048,2048]{1,0:T(8,128)(2,1)} async-done(((bf16[256,2048]{1,0:T(8,128)(2,1)}), bf16[2048,2048]{1,0:T(8,128)(2,1)}) %all-gather.23.cloned.1.call-update) | async-done | bytes 8388624 | tf_op jit(solution)/shard_map/all_gather | solution.py:38
  560.6 23.2 %multiply_convert_fusion = (bf16[2048,1024]{1,0:T(8,128)(2,1)}, bf16[2048,1024]{1,0:T(8,128)(2,1)}, bf16[2048,1024]{1,0:T(8,128)(2,1)}) fusion(f32[2048,1024]{1,0:T(8,128)} %fusion.93, f32[2048,1024]{1,0:T(8,128)} %fusion.94, bf16[2048,2048]{1,0:T(8,128)(2,1)} %all-gather.23.cloned.1.call-done, bf16[1024,2048]{1,0:T(8,128)(2,1)} %all-gather.21.cloned.1.call-done), kind=kOutput, calls=%fused_computation.26 | convolution fusion | flops 8621391872 | bytes 41943040 | tf_op jit(solution)/shard_map/dot_general | solution.py:34
  583.8 13.9 convolution_convert_fusion.2
  597.8 16.3 %fusion.95 = f32[2048,2048]{1,0:T(8,128)} fusion(bf16[2048,1024]{1,0:T(8,128)(2,1)} %get-tuple-element.24, bf16[2048,1024]{1,0:T(8,128)(2,1)} %all-gather.17.cloned.1.call-done), kind=kOutput, calls=%fused_computation.167 | convolution fusion | flops 8589934592 | bytes 25165824 | tf_op jit(solution)/shard_map/dot_general | solution.py:34
  614.1 16.1 %add_convert_fusion = bf16[2048,2048]{1,0:T(8,128)(2,1)} fusion(f32[2048,2048]{1,0:T(8,128)} %fusion.95, bf16[2048,1024]{1,0:T(8,128)(2,1)} %get-tuple-element.23, bf16[2048,1024]{1,0:T(8,128)(2,1)S(1)} %copy-done.41), kind=kOutput, calls=%fused_computation.24 | convolution fusion | flops 8598323200 | bytes 33554432 | tf_op jit(solution)/shard_map/dot_general | solution.py:34
  630.5 38.7 %reduce-scatter.9.cloned.1.call-done = bf16[256,2048]{1,0:T(8,128)(2,1)} async-done(((bf16[2048,2048]{1,0:T(8,128)(2,1)}), bf16[256,2048]{1,0:T(8,128)(2,1)}) %reduce-scatter.9.cloned.1.call-update) | async-done | bytes 1048592 | tf_op jit(solution)/shard_map/reduce_scatter | solution.py:42
  669.1 75.0 %reduce-scatter.11.cloned.1.call-done = bf16[256,2048]{1,0:T(8,128)(2,1)} async-done(((bf16[2048,2048]{1,0:T(8,128)(2,1)}), bf16[256,2048]{1,0:T(8,128)(2,1)}) %reduce-scatter.11.cloned.1.call-update) | async-done | bytes 1048592 | tf_op jit(solution)/shard_map/reduce_scatter | solution.py:42
  744.1 4.4 fusion.34
  749.2 6.5 convolution_convert_fusion.8
  755.8 17.9 %all_to_all.57 = bf16[256,8,256]{2,0,1:T(8,128)(2,1)S(1)} all-to-all(bf16[256,8,256]{2,0,1:T(8,128)(2,1)S(1)} %bitcast.293), channel_id=1, replica_groups=mesh['grp'=4,'chip'=4,'core'=2] {'chip','core'}, dimensions={1} | all-to-all | bytes 2097152 | tf_op jit(solution)/shard_map/all_to_all | solution.py:177
  775.1 3.6 fusion.54
  779.3 3.3 fusion.16
  782.6 26.2 %fusion = (f32[16,4,128]{2,1,0:T(4,128)S(1)}, f32[1024,16,128,4]{2,0,3,1:T(8,128)}) fusion(f32[16,4,128]{2,1,0:T(4,128)S(1)} %copy-done.26, f32[16,4,128]{2,1,0:T(4,128)S(1)} %copy-done.22, f32[1024,16,128,4]{2,0,3,1:T(8,128)} %copy-done, pred[16,1024]{1,0:T(8,128)(4,1)S(1)} %copy-done.24, bf16[16,128,4,64]{1,3,2,0:T(8,128)(2,1)S(1)} %bitcast.316, ...), kind=kOutput, calls=%fused_computation.7 | convolution fusion | flops 1124065280 | bytes 68403200 | tf_op jit(solution)/shard_map/gbikpd,gjkd->gbkpij/dot_general | solution.py:180
  808.8 14.7 %fusion.65 = bf16[1,1024,64]{1,2,0:T(8,128)(2,1)S(1)} fusion(bf16[16,128,4,64]{1,3,2,0:T(8,128)(2,1)S(1)} %bitcast.317, f32[1,1024,64]{1,0,2:T(1,128)S(1)} %slice.91, f32[16,4,128]{2,1,0:T(4,128)S(1)} %copy-done.26, f32[16,4,128]{2,1,0:T(4,128)S(1)} %copy-done.22, f32[1024,16,128,4]{2,0,3,1:T(8,128)} %copy-done, pred[16,1024]{1,0:T(8,128)(4,1)S(1)} %copy-done.24), kind=kOutput, calls=%fused_computation.107 | convolution fusion | flops 1115815936 | bytes 35078144 | tf_op jit(solution)/shard_map/gbkpij,gbikpd->gjkd/dot_general | solution.py:193
  823.8 28.1 %fusion.9 = bf16[16,4,128,1024]{2,3,1,0:T(8,128)(2,1)} fusion(f32[1024,16,128,4]{2,0,3,1:T(8,128)} %get-tuple-element.41, f32[16,4,128]{2,1,0:T(4,128)S(1)} %add.149, f32[16,4,128]{2,1,0:T(4,128)S(1)} %copy-done.26, f32[16,4,128]{2,1,0:T(4,128)S(1)} %copy-done.22, f32[1024,16,128,4]{2,0,3,1:T(8,128)} %copy-done, pred[16,1024]{1,0:T(8,128)(4,1)S(1)} %copy-done.24), kind=kLoop, calls=%fused_computation.19 | loop fusion | flops 58720256 | bytes 84000768 | tf_op jit(solution)/shard_map/reshape.53
  851.9 5.1 fusion.39
  858.9 10.1 fusion.79
  869.0 10.9 fusion.61
  879.9 3.1 fusion.41
  883.0 1.5 copy.214
  886.6 1.4 pad_maximum_fusion.1
  889.0 8.7 convolution_convert_fusion.1
  897.8 14.3 %convolution_convert_fusion.3 = bf16[1024,2048]{1,0:T(8,128)(2,1)} fusion(bf16[2048,1024]{1,0:T(8,128)(2,1)} %get-tuple-element.25, bf16[2048,2048]{1,0:T(8,128)(2,1)} %all-gather.23.cloned.1.call-done), kind=kOutput, calls=%fused_computation.46 | convolution fusion | flops 8592031744 | bytes 16777216 | tf_op jit(solution)/shard_map/dot_general | solution.py:30
  912.2 14.3 %convolution_convert_fusion.4 = bf16[2048,1024]{1,0:T(8,128)(2,1)} fusion(bf16[2048,2048]{1,0:T(8,128)(2,1)} %all-gather.15.cloned.1.call-done, bf16[2048,1024]{1,0:T(8,128)(2,1)} %get-tuple-element.23), kind=kOutput, calls=%fused_computation.47 | convolution fusion | flops 8592031744 | bytes 16777216 | tf_op jit(solution)/shard_map/dot_general | solution.py:30
  926.5 14.5 %convolution_convert_fusion.5 = bf16[2048,1024]{1,0:T(8,128)(2,1)} fusion(bf16[2048,2048]{1,0:T(8,128)(2,1)} %all-gather.15.cloned.1.call-done, bf16[2048,1024]{1,0:T(8,128)(2,1)} %get-tuple-element.24), kind=kOutput, calls=%fused_computation.48 | convolution fusion | flops 8592031744 | bytes 16777216 | tf_op jit(solution)/shard_map/dot_general | solution.py:30
  942.5 8.7 convolution_convert_fusion.6
  951.1 17.2 %reduce-scatter.13.cloned.1.call-done = bf16[256,2048]{1,0:T(8,128)(2,1)} async-done(((bf16[2048,2048]{1,0:T(8,128)(2,1)}), bf16[256,2048]{1,0:T(8,128)(2,1)}) %reduce-scatter.13.cloned.1.call-update) | async-done | bytes 1048592 | tf_op jit(solution)/shard_map/reduce_scatter | solution.py:42
  968.3 1.9 fusion.38
  970.3 3.0 pad_maximum_fusion
  973.6 6.8 convolution_convert_fusion
  980.5 66.9 %reduce-scatter.23.cloned.1.call-done = bf16[256,2048]{1,0:T(8,128)(2,1)} async-done(((bf16[1024,2048]{1,0:T(8,128)(2,1)}), bf16[256,2048]{1,0:T(8,128)(2,1)}) %reduce-scatter.23.cloned.1.call-update) | async-done | bytes 1048592 | tf_op jit(solution)/shard_map/reduce_scatter | solution.py:42
  1047.3 2.8 convert_element_type.174
  1050.1 76.8 %reduce-scatter.21.cloned.1.call-done = bf16[2048,256]{1,0:T(8,128)(2,1)} async-done(((bf16[2048,1024]{1,0:T(8,128)(2,1)}), bf16[2048,256]{1,0:T(8,128)(2,1)}) %reduce-scatter.21.cloned.1.call-update) | async-done | bytes 1048592 | tf_op jit(solution)/shard_map/reduce_scatter | solution.py:42
  1126.9 2.7 convert_element_type.172
  1129.6 2.0 pad_maximum_fusion.5
  1131.7 74.8 %reduce-scatter.19.cloned.1.call-done = bf16[2048,256]{1,0:T(8,128)(2,1)} async-done(((bf16[2048,1024]{1,0:T(8,128)(2,1)}), bf16[2048,256]{1,0:T(8,128)(2,1)}) %reduce-scatter.19.cloned.1.call-update) | async-done | bytes 1048592 | tf_op jit(solution)/shard_map/reduce_scatter | solution.py:42
  1206.5 2.7 convert_element_type.170
  1209.2 44.4 %psum.7 = f32[3]{0:T(128)S(1)} all-reduce(f32[3]{0:T(128)S(1)} %pad_maximum_fusion.5), channel_id=1, replica_groups=mesh['grp'=4,'chip'=4,'core'=2] {'grp','chip','core'}, use_global_device_ids=true, to_apply=%region_27.28 | all-reduce | flops 3 | bytes 24 | tf_op jit(solution)/shard_map/psum | solution.py:240
  1254.1 2.1 copy.217
  1256.1 4.1 all-to-all-start.3
  1260.3 2.8 fusion.29
  1263.1 140.9 %reduce-scatter.17.cloned.1.call-done = bf16[64,2048]{1,0:T(8,128)(2,1)} async-done(((bf16[2048,2048]{1,0:T(8,128)(2,1)}), bf16[64,2048]{1,0:T(8,128)(2,1)}) %reduce-scatter.17.cloned.1.call-update) | async-done | bytes 262160 | tf_op jit(solution)/shard_map/reduce_scatter | solution.py:42
  1404.0 1.8 convert_element_type.168
  (190 shorter events, 34.1 us)
Async XLA Ops:
  7.2 21.2 %copy-start.39 = (s32[64]{0:T(128)S(1)}, s32[64]{0:T(128)}, u32[]{:S(2)}) copy-start(s32[64]{0:T(128)} %param.15) | copy-start | bytes 772
  7.2 21.2 %copy-start.40 = (s32[64]{0:T(128)S(1)}, s32[64]{0:T(128)}, u32[]{:S(2)}) copy-start(s32[64]{0:T(128)} %param.14) | copy-start | bytes 772
  7.2 64.5 %all-gather.11.cloned.1.call-start = ((), (), s32[]{:S(2)}) async-start(), calls=%async_computation.13 | async-start | bytes 2621440 | tf_op jit(solution)/shard_map/all_gather | solution.py:38
  26.2 100.5 %all-gather.9.cloned.1.call-start = ((), (), s32[]{:S(2)}) async-start(), calls=%async_computation.12 | async-start | bytes 9437184 | tf_op jit(solution)/shard_map/all_gather | solution.py:38
  27.0 183.8 %all-gather.13.cloned.1.call-start = ((), (), s32[]{:S(2)}) async-start(), calls=%async_computation.14 | async-start | bytes 8650752 | tf_op jit(solution)/shard_map/all_gather | solution.py:38
  27.7 260.0 %all-gather.19.cloned.1.call-start = ((), (), s32[]{:S(2)}) async-start(), calls=%async_computation.17 | async-start | bytes 5242880 | tf_op jit(solution)/shard_map/all_gather | solution.py:38
  28.3 314.3 %all-gather.15.cloned.1.call-start = ((), (), s32[]{:S(2)}) async-start(), calls=%async_computation.15 | async-start | bytes 9437184 | tf_op jit(solution)/shard_map/all_gather | solution.py:38
  28.8 143.8 %copy-start.29 = (pred[128,128]{0,1:T(8,128)(4,1)}, pred[128,128]{0,1:T(8,128)(4,1)S(1)}, u32[]{:S(2)}) copy-start(pred[128,128]{0,1:T(8,128)(4,1)S(1)} %iota_compare_fusion.1) | copy-start | bytes 49156
  28.8 109.9 %copy-start.38 = (s32[1024]{0:T(1024)}, s32[1024]{0:T(1024)S(1)}, u32[]{:S(2)}) copy-start(s32[1024]{0:T(1024)S(1)} %pad_clamp_fusion.1) | copy-start | bytes 12292
  28.8 161.3 %copy-start.37 = (s32[1024]{0:T(1024)}, s32[1024]{0:T(1024)S(1)}, u32[]{:S(2)}) copy-start(s32[1024]{0:T(1024)S(1)} %pad_clamp_fusion) | copy-start | bytes 12292
  28.9 144.9 %copy-start.23 = (pred[16,1024]{1,0:T(8,128)(4,1)}, pred[16,1024]{1,0:T(8,128)(4,1)S(1)}, u32[]{:S(2)}) copy-start(pred[16,1024]{1,0:T(8,128)(4,1)S(1)} %iota_compare_fusion.2) | copy-start | bytes 49156
  73.5 58.5 %copy-start.31 = (f32[2048]{0:T(1024)}, f32[2048]{0:T(1024)S(1)}, u32[]{:S(2)}) copy-start(f32[2048]{0:T(1024)S(1)} %get-tuple-element.18) | copy-start | bytes 24580
  126.7 5.8 copy-start.9
  132.0 6.8 copy-start.35
  141.1 1.8 copy-start.12
  141.3 1.5 copy-start.18
  147.4 9.3 copy-start.3
  147.5 4.0 copy-start.13
  156.8 15.8 %copy-start = (f32[1024,16,128,4]{2,0,3,1:T(8,128)}, f32[1024,16,128,4]{2,0,3,1:T(8,128)S(1)}, u32[]{:S(2)}) copy-start(f32[1024,16,128,4]{2,0,3,1:T(8,128)S(1)} %get-tuple-element.37) | copy-start | bytes 100663296
  156.8 17.1 %copy-start.21 = (f32[16,4,128]{2,1,0:T(4,128)}, f32[16,4,128]{2,1,0:T(4,128)S(1)}, u32[]{:S(2)}) copy-start(f32[16,4,128]{2,1,0:T(4,128)S(1)} %max.8) | copy-start | bytes 98308
  163.3 9.3 copy-start.1
  163.3 9.3 copy-start.27
  172.6 1.3 copy-start.25
  172.6 1.3 copy-start.19
  189.6 21.1 %copy-start.7 = (bf16[256,2048]{1,0:T(8,128)(2,1)S(1)}, bf16[256,2048]{1,0:T(8,128)(2,1)}, u32[]{:S(2)}) copy-start(bf16[256,2048]{1,0:T(8,128)(2,1)} %param.13) | copy-start | bytes 3145732
  218.3 2.6 copy-start.10
  219.5 205.1 %all-gather.17.cloned.1.call-start = ((), (), s32[]{:S(2)}) async-start(), calls=%async_computation.16 | async-start | bytes 5242880 | tf_op jit(solution)/shard_map/all_gather | solution.py:38
  220.1 285.1 %all-gather.21.cloned.1.call-start = ((), (), s32[]{:S(2)}) async-start(), calls=%async_computation.18 | async-start | bytes 5242880 | tf_op jit(solution)/shard_map/all_gather | solution.py:38
  220.8 339.7 %all-gather.23.cloned.1.call-start = ((), (), s32[]{:S(2)}) async-start(), calls=%async_computation.20 | async-start | bytes 9437184 | tf_op jit(solution)/shard_map/all_gather | solution.py:38
  222.1 447.0 %reduce-scatter.9.cloned.1.call-start = ((), (), s32[]{:S(2)}) async-start(), calls=%async_computation.19 | async-start | bytes 9437184 | tf_op jit(solution)/shard_map/reduce_scatter | solution.py:42
  597.7 146.4 %reduce-scatter.11.cloned.1.call-start = ((), (), s32[]{:S(2)}) async-start(), calls=%async_computation.21 | async-start | bytes 9437184 | tf_op jit(solution)/shard_map/reduce_scatter | solution.py:42
  597.8 16.4 %copy-start.41 = (bf16[2048,1024]{1,0:T(8,128)(2,1)S(1)}, bf16[2048,1024]{1,0:T(8,128)(2,1)}, u32[]{:S(2)}) copy-start(bf16[2048,1024]{1,0:T(8,128)(2,1)} %all-gather.19.cloned.1.call-done) | copy-start | bytes 12582916
  630.2 338.1 %reduce-scatter.13.cloned.1.call-start = ((), (), s32[]{:S(2)}) async-start(), calls=%async_computation.22 | async-start | bytes 9437184 | tf_op jit(solution)/shard_map/reduce_scatter | solution.py:42
  744.1 4.5 copy-start.11
  749.1 6.5 copy-start.5
  755.7 19.4 %copy-start.22 = (f32[16,4,128]{2,1,0:T(4,128)S(1)}, f32[16,4,128]{2,1,0:T(4,128)}, u32[]{:S(2)}) copy-start(f32[16,4,128]{2,1,0:T(4,128)} %copy-done.21) | copy-start | bytes 98308
  755.7 19.4 %copy-start.26 = (f32[16,4,128]{2,1,0:T(4,128)S(1)}, f32[16,4,128]{2,1,0:T(4,128)}, u32[]{:S(2)}) copy-start(f32[16,4,128]{2,1,0:T(4,128)} %copy-done.25) | copy-start | bytes 98308
  755.7 19.4 %copy-start.30 = (pred[128,128]{0,1:T(8,128)(4,1)S(1)}, pred[128,128]{0,1:T(8,128)(4,1)}, u32[]{:S(2)}) copy-start(pred[128,128]{0,1:T(8,128)(4,1)} %copy-done.29) | copy-start | bytes 49156
  775.1 4.1 copy-start.2
  775.1 4.1 copy-start.28
  779.3 3.3 copy-start.20
  779.3 3.3 copy-start.24
  851.9 5.1 copy-start.4
  857.0 1.9 copy-start.14
  869.0 10.9 copy-start.15
  889.0 8.7 copy-start.16
  897.8 149.6 %reduce-scatter.23.cloned.1.call-start = ((), (), s32[]{:S(2)}) async-start(), calls=%async_computation.27 | async-start | bytes 5242880 | tf_op jit(solution)/shard_map/reduce_scatter | solution.py:42
  912.1 214.8 %reduce-scatter.21.cloned.1.call-start = ((), (), s32[]{:S(2)}) async-start(), calls=%async_computation.26 | async-start | bytes 5242880 | tf_op jit(solution)/shard_map/reduce_scatter | solution.py:42
  926.5 280.0 %reduce-scatter.19.cloned.1.call-start = ((), (), s32[]{:S(2)}) async-start(), calls=%async_computation.25 | async-start | bytes 5242880 | tf_op jit(solution)/shard_map/reduce_scatter | solution.py:42
  941.0 0.7 copy-start.34
  941.0 0.7 copy-start.33
  941.0 1.4 copy-start.17
  941.0 1.4 copy-start.32
  941.1 1.4 copy-start.36
  941.1 313.0 %reduce-scatter.15.cloned.1.call-start = ((), (), s32[]{:S(2)}) async-start(), calls=%async_computation.23 | async-start | bytes 2621440 | tf_op jit(solution)/shard_map/reduce_scatter | solution.py:42
  942.5 25.9 %copy-start.8 = (bf16[256,2048]{1,0:T(8,128)(2,1)S(1)}, bf16[256,2048]{1,0:T(8,128)(2,1)}, u32[]{:S(2)}) copy-start(bf16[256,2048]{1,0:T(8,128)(2,1)} %param.13) | copy-start | bytes 3145732
  951.1 22.5 %copy-start.6 = (f32[256,2048]{1,0:T(8,128)S(1)}, f32[256,2048]{1,0:T(8,128)}, u32[]{:S(2)}) copy-start(f32[256,2048]{1,0:T(8,128)} %copy-done.5) | copy-start | bytes 6291460
  973.3 430.7 %reduce-scatter.17.cloned.1.call-start = ((), (), s32[]{:S(2)}) async-start(), calls=%async_computation.24 | async-start | bytes 8650752 | tf_op jit(solution)/shard_map/reduce_scatter | solution.py:42
  1256.1 149.7 %all-to-all-start.3 = ((bf16[8,64,512]{2,1,0:T(8,128)(2,1)}), bf16[8,64,512]{2,1,0:T(8,128)(2,1)}, u32[]{:S(2)}, u32[]{:S(2)}) async-start(bf16[8,64,512]{2,1,0:T(8,128)(2,1)} %bitcast.303), calls=%async_computation.7 | async-start | bytes 1048576 | tf_op jit(solution)/shard_map/all_to_all | solution.py:220
Sparse Core Ops, SparseCore 0:
  26.3 45.2 all-gather.10
  73.5 53.1 all-gather.8
  129.6 77.4 all-gather.12
  208.5 79.1 all-gather.18
  290.0 52.5 all-gather.14
  344.0 80.5 all-gather.16
  426.2 78.9 all-gather.20
  507.6 52.9 all-gather.22
  597.8 71.2 reduce-scatter.8
  672.8 71.2 reduce-scatter.10
  897.9 70.3 reduce-scatter.12
  970.6 76.7 reduce-scatter.22
  1049.6 77.2 reduce-scatter.20
  1129.2 77.2 reduce-scatter.18
  1208.6 45.3 reduce-scatter.14
  1256.3 147.6 reduce-scatter.16
where the time goes:
time: 1430 us; the launch traced here: 1420 us
  waiting for transfers between devices  899 us (63%)
  matrix products  285 us (20%)
  blocking collectives  95.7 us (7%)
  other arithmetic  87.5 us (6%)
  local copies, waits for them, and re-layouts  29.8 us (2%)
  between operations  15.2 us (1%)
    reduce_scatter x8, waiting for transfers between devices, scatter(): return lax.psum_scatter(values, axes, scatter_dimension=axis, tiled=True)  490 us
    all_gather x8, waiting for transfers between devices, gather(): return lax.all_gather(values, axes, axis=axis, tiled=True)  405 us
    dot_general x5, matrix products, over_cols(): lax.dot_general(left, right, (((1,), (1,)), ((), ())), preferred_element_...  70.8 us
    dot_general x5, matrix products, over_rows(): lax.dot_general(left, right, (((0,), (0,)), ((), ())), preferred_element_...  58.6 us
    dot_general x5, matrix products, matmul(): return jnp.dot(left, right, preferred_element_type=F32)  56.9 us
    psum x1, blocking collectives, on_device(): totals = lax.psum(squares, EVERY)  44.4 us
    another operation x3, other arithmetic  33.2 us
  transfers between devices with their start and end apart: 17, of which 14 were waited for; matrix products, arithmetic and copies ran while one was open for 15% of the time, Pallas kernels for 0%

commit v1 on v0

--- a/solution.py
+++ b/solution.py
@@ -237,7 +237,7 @@
             jnp.sum(scaled_mlp * scaled_mlp),
         ]
     )
-    totals = lax.psum(squares, EVERY)
+    totals = jax.lax.psum(jax.lax.psum(squares, ("chip", "core")), "grp")
     rms_stats = jnp.sqrt(totals / (rows * grps * devs * D))
     return (
         layer_out.astype(BF16),

time: 1430 us -> 1430 us (level)
  blocking collectives: 95.7 us -> 76.3 us
  waiting for transfers between devices: 899 us -> 917 us
    psum x1 -> x2, blocking collectives: 44.4 us -> 25 us  [on_device(): totals = jax.lax.psum(jax.lax.psum(squares, ('chip', 'core')), 'grp')]
    reduce_scatter x8, waiting for transfers between devices: 490 us -> 509 us  [scatter(): return lax.psum_scatter(values, axes, scatter_dimension=axis, tiled=True)]
  transfers between devices with their start and end apart: 17 -> 17, of which waited for: 14 -> 15; matrix products, arithmetic and copies ran while one was open for 15% -> 16% of each run, Pallas kernels for 0% -> 0%
where the time goes in v1:
time: 1430 us; the launch traced here: 1420 us
  waiting for transfers between devices  917 us (64%)
  matrix products  285 us (20%)
  other arithmetic  87.3 us (6%)
  blocking collectives  76.3 us (5%)
  local copies, waits for them, and re-layouts  30.2 us (2%)
  between operations  15.1 us (1%)
    reduce_scatter x8, waiting for transfers between devices, scatter(): return lax.psum_scatter(values, axes, scatter_dimension=axis, tiled=True)  509 us
    all_gather x8, waiting for transfers between devices, gather(): return lax.all_gather(values, axes, axis=axis, tiled=True)  405 us
    dot_general x5, matrix products, over_cols(): lax.dot_general(left, right, (((1,), (1,)), ((), ())), preferred_element_...  70.9 us
    dot_general x5, matrix products, over_rows(): lax.dot_general(left, right, (((0,), (0,)), ((), ())), preferred_element_...  58.7 us
    dot_general x5, matrix products, matmul(): return jnp.dot(left, right, preferred_element_type=F32)  56.7 us
    another operation x3, other arithmetic  33 us
  transfers between devices with their start and end apart: 17, of which 15 were waited for; matrix products, arithmetic and copies ran while one was open for 16% of the time, Pallas kernels for 0%

profile of v1, /device:TPU:0, one launch (start us, length us, event | category | flops | bytes accessed | tf_op | source)
XLA Modules:
  0.0 1416.5 jit_solution(10884366551526619123)
XLA Ops:
  11.4 14.8 %all_to_all.55 = bf16[64,8,512]{2,0,1:T(8,128)(2,1)} all-to-all(bf16[64,8,512]{2,0,1:T(8,128)(2,1)S(1)} %copy.186), channel_id=1, replica_groups=mesh['grp'=4,'chip'=4,'core'=2] {'chip','core'}, dimensions={1} | all-to-all | bytes 1048576 | tf_op jit(solution)/shard_map/all_to_all | solution.py:101
  28.9 42.7 %all-gather.11.cloned.1.call-done = bf16[2048,512]{1,0:T(8,128)(2,1)} async-done(((bf16[512,512]{1,0:T(8,128)(2,1)}), bf16[2048,512]{1,0:T(8,128)(2,1)}) %all-gather.11.cloned.1.call-update) | async-done | bytes 2097168 | tf_op jit(solution)/shard_map/all_gather | solution.py:38
  71.7 1.8 convert_reduce_fusion
  73.5 53.2 %all-gather.9.cloned.1.call-done = bf16[2048,2048]{1,0:T(8,128)(2,1)} async-done(((bf16[256,2048]{1,0:T(8,128)(2,1)}), bf16[2048,2048]{1,0:T(8,128)(2,1)}) %all-gather.9.cloned.1.call-update) | async-done | bytes 8388624 | tf_op jit(solution)/shard_map/all_gather | solution.py:38
  126.7 5.2 fusion.6
  132.5 6.2 convolution_convert_fusion.7
  142.9 3.8 reshape.454
  147.8 4.0 fusion.21
  151.8 5.3 fusion.5
  157.1 6.5 fusion.20
  163.7 9.2 fusion.4
  174.2 15.8 %fusion.42 = bf16[1,16,128,1,4,64]{2,5,4,1,3,0:T(8,128)(2,1)S(1)} fusion(f32[16,64,4,128]{3,1,2,0:T(8,128)S(1)} %fusion.45, bf16[1,2048,1,64]{1,3,2,0:T(8,128)(2,1)S(1)} %bitcast.311, f32[16,4,128]{2,1,0:T(4,128)S(1)} %add.140, f32[16,4,128]{2,1,0:T(4,128)S(1)} %max.8, f32[1024,16,128,4]{2,0,3,1:T(8,128)} %copy-done, ...), kind=kOutput, calls=%fused_computation.82 | convolution fusion | flops 1116733440 | bytes 36913152 | tf_op jit(solution)/shard_map/gbkpij,gjkd->gbikpd/dot_general | solution.py:139
  191.2 18.5 %all_to_all.56 = bf16[8,256,256]{2,1,0:T(8,128)(2,1)S(1)} all-to-all(bf16[8,256,256]{2,1,0:T(8,128)(2,1)S(1)} %bitcast.291), channel_id=1, replica_groups=mesh['grp'=4,'chip'=4,'core'=2] {'chip','core'}, dimensions={0} | all-to-all | bytes 2097152 | tf_op jit(solution)/shard_map/all_to_all | solution.py:143
  211.1 7.6 multiply_reduce_fusion.3
  222.6 65.1 %all-gather.19.cloned.1.call-done = bf16[2048,1024]{1,0:T(8,128)(2,1)} async-done(((bf16[2048,256]{1,0:T(8,128)(2,1)}), bf16[2048,1024]{1,0:T(8,128)(2,1)}) %all-gather.19.cloned.1.call-update) | async-done | bytes 4194320 | tf_op jit(solution)/shard_map/all_gather | solution.py:38
  287.7 54.9 %all-gather.15.cloned.1.call-done = bf16[2048,2048]{1,0:T(8,128)(2,1)} async-done(((bf16[256,2048]{1,0:T(8,128)(2,1)}), bf16[2048,2048]{1,0:T(8,128)(2,1)}) %all-gather.15.cloned.1.call-update) | async-done | bytes 8388624 | tf_op jit(solution)/shard_map/all_gather | solution.py:38
  342.6 14.5 %fusion.94 = f32[2048,1024]{1,0:T(8,128)} fusion(bf16[2048,2048]{1,0:T(8,128)(2,1)} %all-gather.15.cloned.1.call-done, bf16[2048,1024]{1,0:T(8,128)(2,1)} %all-gather.19.cloned.1.call-done), kind=kOutput, calls=%fused_computation.166 | convolution fusion | flops 8589934592 | bytes 20971520 | tf_op jit(solution)/shard_map/dot_general | solution.py:26
  357.1 67.5 %all-gather.17.cloned.1.call-done = bf16[2048,1024]{1,0:T(8,128)(2,1)} async-done(((bf16[2048,256]{1,0:T(8,128)(2,1)}), bf16[2048,1024]{1,0:T(8,128)(2,1)}) %all-gather.17.cloned.1.call-update) | async-done | bytes 4194320 | tf_op jit(solution)/shard_map/all_gather | solution.py:38
  424.6 14.4 %fusion.93 = f32[2048,1024]{1,0:T(8,128)} fusion(bf16[2048,2048]{1,0:T(8,128)(2,1)} %all-gather.15.cloned.1.call-done, bf16[2048,1024]{1,0:T(8,128)(2,1)} %all-gather.17.cloned.1.call-done), kind=kOutput, calls=%fused_computation.165 | convolution fusion | flops 8589934592 | bytes 20971520 | tf_op jit(solution)/shard_map/dot_general | solution.py:26
  439.0 66.1 %all-gather.21.cloned.1.call-done = bf16[1024,2048]{1,0:T(8,128)(2,1)} async-done(((bf16[256,2048]{1,0:T(8,128)(2,1)}), bf16[1024,2048]{1,0:T(8,128)(2,1)}) %all-gather.21.cloned.1.call-update) | async-done | bytes 4194320 | tf_op jit(solution)/shard_map/all_gather | solution.py:38
  505.2 55.4 %all-gather.23.cloned.1.call-done = bf16[2048,2048]{1,0:T(8,128)(2,1)} async-done(((bf16[256,2048]{1,0:T(8,128)(2,1)}), bf16[2048,2048]{1,0:T(8,128)(2,1)}) %all-gather.23.cloned.1.call-update) | async-done | bytes 8388624 | tf_op jit(solution)/shard_map/all_gather | solution.py:38
  560.6 23.2 %multiply_convert_fusion = (bf16[2048,1024]{1,0:T(8,128)(2,1)}, bf16[2048,1024]{1,0:T(8,128)(2,1)}, bf16[2048,1024]{1,0:T(8,128)(2,1)}) fusion(f32[2048,1024]{1,0:T(8,128)} %fusion.93, f32[2048,1024]{1,0:T(8,128)} %fusion.94, bf16[2048,2048]{1,0:T(8,128)(2,1)} %all-gather.23.cloned.1.call-done, bf16[1024,2048]{1,0:T(8,128)(2,1)} %all-gather.21.cloned.1.call-done), kind=kOutput, calls=%fused_computation.26 | convolution fusion | flops 8621391872 | bytes 41943040 | tf_op jit(solution)/shard_map/dot_general | solution.py:34
  583.7 13.9 convolution_convert_fusion.2
  597.8 16.5 %fusion.95 = f32[2048,2048]{1,0:T(8,128)} fusion(bf16[2048,1024]{1,0:T(8,128)(2,1)} %get-tuple-element.24, bf16[2048,1024]{1,0:T(8,128)(2,1)} %all-gather.17.cloned.1.call-done), kind=kOutput, calls=%fused_computation.167 | convolution fusion | flops 8589934592 | bytes 25165824 | tf_op jit(solution)/shard_map/dot_general | solution.py:34
  614.3 16.0 %add_convert_fusion = bf16[2048,2048]{1,0:T(8,128)(2,1)} fusion(f32[2048,2048]{1,0:T(8,128)} %fusion.95, bf16[2048,1024]{1,0:T(8,128)(2,1)} %get-tuple-element.23, bf16[2048,1024]{1,0:T(8,128)(2,1)S(1)} %copy-done.41), kind=kOutput, calls=%fused_computation.24 | convolution fusion | flops 8598323200 | bytes 33554432 | tf_op jit(solution)/shard_map/dot_general | solution.py:34
  630.5 38.6 %reduce-scatter.9.cloned.1.call-done = bf16[256,2048]{1,0:T(8,128)(2,1)} async-done(((bf16[2048,2048]{1,0:T(8,128)(2,1)}), bf16[256,2048]{1,0:T(8,128)(2,1)}) %reduce-scatter.9.cloned.1.call-update) | async-done | bytes 1048592 | tf_op jit(solution)/shard_map/reduce_scatter | solution.py:42
  669.1 75.0 %reduce-scatter.11.cloned.1.call-done = bf16[256,2048]{1,0:T(8,128)(2,1)} async-done(((bf16[2048,2048]{1,0:T(8,128)(2,1)}), bf16[256,2048]{1,0:T(8,128)(2,1)}) %reduce-scatter.11.cloned.1.call-update) | async-done | bytes 1048592 | tf_op jit(solution)/shard_map/reduce_scatter | solution.py:42
  744.2 4.4 fusion.34
  749.2 6.5 convolution_convert_fusion.8
  755.8 17.9 %all_to_all.57 = bf16[256,8,256]{2,0,1:T(8,128)(2,1)S(1)} all-to-all(bf16[256,8,256]{2,0,1:T(8,128)(2,1)S(1)} %bitcast.293), channel_id=1, replica_groups=mesh['grp'=4,'chip'=4,'core'=2] {'chip','core'}, dimensions={1} | all-to-all | bytes 2097152 | tf_op jit(solution)/shard_map/all_to_all | solution.py:177
  775.2 3.6 fusion.54
  779.3 3.3 fusion.16
  782.6 26.2 %fusion = (f32[16,4,128]{2,1,0:T(4,128)S(1)}, f32[1024,16,128,4]{2,0,3,1:T(8,128)}) fusion(f32[16,4,128]{2,1,0:T(4,128)S(1)} %copy-done.26, f32[16,4,128]{2,1,0:T(4,128)S(1)} %copy-done.22, f32[1024,16,128,4]{2,0,3,1:T(8,128)} %copy-done, pred[16,1024]{1,0:T(8,128)(4,1)S(1)} %copy-done.24, bf16[16,128,4,64]{1,3,2,0:T(8,128)(2,1)S(1)} %bitcast.316, ...), kind=kOutput, calls=%fused_computation.7 | convolution fusion | flops 1124065280 | bytes 68403200 | tf_op jit(solution)/shard_map/gbikpd,gjkd->gbkpij/dot_general | solution.py:180
  808.9 14.7 %fusion.65 = bf16[1,1024,64]{1,2,0:T(8,128)(2,1)S(1)} fusion(bf16[16,128,4,64]{1,3,2,0:T(8,128)(2,1)S(1)} %bitcast.317, f32[1,1024,64]{1,0,2:T(1,128)S(1)} %slice.91, f32[16,4,128]{2,1,0:T(4,128)S(1)} %copy-done.26, f32[16,4,128]{2,1,0:T(4,128)S(1)} %copy-done.22, f32[1024,16,128,4]{2,0,3,1:T(8,128)} %copy-done, pred[16,1024]{1,0:T(8,128)(4,1)S(1)} %copy-done.24), kind=kOutput, calls=%fused_computation.107 | convolution fusion | flops 1115815936 | bytes 35078144 | tf_op jit(solution)/shard_map/gbkpij,gbikpd->gjkd/dot_general | solution.py:193
  823.9 27.9 %fusion.9 = bf16[16,4,128,1024]{2,3,1,0:T(8,128)(2,1)} fusion(f32[1024,16,128,4]{2,0,3,1:T(8,128)} %get-tuple-element.41, f32[16,4,128]{2,1,0:T(4,128)S(1)} %add.151, f32[16,4,128]{2,1,0:T(4,128)S(1)} %copy-done.26, f32[16,4,128]{2,1,0:T(4,128)S(1)} %copy-done.22, f32[1024,16,128,4]{2,0,3,1:T(8,128)} %copy-done, pred[16,1024]{1,0:T(8,128)(4,1)S(1)} %copy-done.24), kind=kLoop, calls=%fused_computation.19 | loop fusion | flops 58720256 | bytes 84000768 | tf_op jit(solution)/shard_map/reshape.53
  851.8 5.1 fusion.39
  858.7 10.1 fusion.79
  868.8 10.9 fusion.61
  879.8 3.1 fusion.41
  882.9 1.5 copy.214
  888.9 8.7 convolution_convert_fusion.1
  897.7 14.5 %convolution_convert_fusion.3 = bf16[1024,2048]{1,0:T(8,128)(2,1)} fusion(bf16[2048,1024]{1,0:T(8,128)(2,1)} %get-tuple-element.25, bf16[2048,2048]{1,0:T(8,128)(2,1)} %all-gather.23.cloned.1.call-done), kind=kOutput, calls=%fused_computation.46 | convolution fusion | flops 8592031744 | bytes 16777216 | tf_op jit(solution)/shard_map/dot_general | solution.py:30
  912.2 14.2 %convolution_convert_fusion.4 = bf16[2048,1024]{1,0:T(8,128)(2,1)} fusion(bf16[2048,2048]{1,0:T(8,128)(2,1)} %all-gather.15.cloned.1.call-done, bf16[2048,1024]{1,0:T(8,128)(2,1)} %get-tuple-element.23), kind=kOutput, calls=%fused_computation.47 | convolution fusion | flops 8592031744 | bytes 16777216 | tf_op jit(solution)/shard_map/dot_general | solution.py:30
  926.5 14.5 %convolution_convert_fusion.5 = bf16[2048,1024]{1,0:T(8,128)(2,1)} fusion(bf16[2048,2048]{1,0:T(8,128)(2,1)} %all-gather.15.cloned.1.call-done, bf16[2048,1024]{1,0:T(8,128)(2,1)} %get-tuple-element.24), kind=kOutput, calls=%fused_computation.48 | convolution fusion | flops 8592031744 | bytes 16777216 | tf_op jit(solution)/shard_map/dot_general | solution.py:30
  942.4 8.7 convolution_convert_fusion.6
  951.1 17.0 %reduce-scatter.13.cloned.1.call-done = bf16[256,2048]{1,0:T(8,128)(2,1)} async-done(((bf16[2048,2048]{1,0:T(8,128)(2,1)}), bf16[256,2048]{1,0:T(8,128)(2,1)}) %reduce-scatter.13.cloned.1.call-update) | async-done | bytes 1048592 | tf_op jit(solution)/shard_map/reduce_scatter | solution.py:42
  968.1 1.9 fusion.38
  970.1 3.0 pad_maximum_fusion
  973.4 6.8 convolution_convert_fusion
  980.2 67.0 %reduce-scatter.23.cloned.1.call-done = bf16[256,2048]{1,0:T(8,128)(2,1)} async-done(((bf16[1024,2048]{1,0:T(8,128)(2,1)}), bf16[256,2048]{1,0:T(8,128)(2,1)}) %reduce-scatter.23.cloned.1.call-update) | async-done | bytes 1048592 | tf_op jit(solution)/shard_map/reduce_scatter | solution.py:42
  1047.2 2.8 convert_element_type.174
  1050.0 2.0 pad_maximum_fusion.5
  1052.0 74.8 %reduce-scatter.21.cloned.1.call-done = bf16[2048,256]{1,0:T(8,128)(2,1)} async-done(((bf16[2048,1024]{1,0:T(8,128)(2,1)}), bf16[2048,256]{1,0:T(8,128)(2,1)}) %reduce-scatter.21.cloned.1.call-update) | async-done | bytes 1048592 | tf_op jit(solution)/shard_map/reduce_scatter | solution.py:42
  1126.8 2.7 convert_element_type.172
  1129.5 14.0 psum.14
  1143.5 62.8 %reduce-scatter.19.cloned.1.call-done = bf16[2048,256]{1,0:T(8,128)(2,1)} async-done(((bf16[2048,1024]{1,0:T(8,128)(2,1)}), bf16[2048,256]{1,0:T(8,128)(2,1)}) %reduce-scatter.19.cloned.1.call-update) | async-done | bytes 1048592 | tf_op jit(solution)/shard_map/reduce_scatter | solution.py:42
  1206.3 2.7 convert_element_type.170
  1209.0 11.0 psum.15
  1220.6 32.4 %reduce-scatter.15.cloned.1.call-done = bf16[512,512]{0,1:T(8,128)(2,1)} async-done(((bf16[2048,512]{0,1:T(8,128)(2,1)}), bf16[512,512]{0,1:T(8,128)(2,1)}) %reduce-scatter.15.cloned.1.call-update) | async-done | bytes 524304 | tf_op jit(solution)/shard_map/reduce_scatter | solution.py:42
  1252.9 2.0 copy.217
  1255.0 4.2 all-to-all-start.3
  1259.1 2.8 fusion.29
  1261.9 141.3 %reduce-scatter.17.cloned.1.call-done = bf16[64,2048]{1,0:T(8,128)(2,1)} async-done(((bf16[2048,2048]{1,0:T(8,128)(2,1)}), bf16[64,2048]{1,0:T(8,128)(2,1)}) %reduce-scatter.17.cloned.1.call-update) | async-done | bytes 262160 | tf_op jit(solution)/shard_map/reduce_scatter | solution.py:42
  1403.2 1.8 convert_element_type.168
  (191 shorter events, 36.8 us)
Async XLA Ops:
  7.2 21.2 %copy-start.39 = (s32[64]{0:T(128)S(1)}, s32[64]{0:T(128)}, u32[]{:S(2)}) copy-start(s32[64]{0:T(128)} %param.15) | copy-start | bytes 772
  7.2 21.2 %copy-start.40 = (s32[64]{0:T(128)S(1)}, s32[64]{0:T(128)}, u32[]{:S(2)}) copy-start(s32[64]{0:T(128)} %param.14) | copy-start | bytes 772
  7.2 64.5 %all-gather.11.cloned.1.call-start = ((), (), s32[]{:S(2)}) async-start(), calls=%async_computation.13 | async-start | bytes 2621440 | tf_op jit(solution)/shard_map/all_gather | solution.py:38
  26.2 100.5 %all-gather.9.cloned.1.call-start = ((), (), s32[]{:S(2)}) async-start(), calls=%async_computation.12 | async-start | bytes 9437184 | tf_op jit(solution)/shard_map/all_gather | solution.py:38
  27.0 184.1 %all-gather.13.cloned.1.call-start = ((), (), s32[]{:S(2)}) async-start(), calls=%async_computation.14 | async-start | bytes 8650752 | tf_op jit(solution)/shard_map/all_gather | solution.py:38
  27.7 260.0 %all-gather.19.cloned.1.call-start = ((), (), s32[]{:S(2)}) async-start(), calls=%async_computation.17 | async-start | bytes 5242880 | tf_op jit(solution)/shard_map/all_gather | solution.py:38
  28.3 314.3 %all-gather.15.cloned.1.call-start = ((), (), s32[]{:S(2)}) async-start(), calls=%async_computation.15 | async-start | bytes 9437184 | tf_op jit(solution)/shard_map/all_gather | solution.py:38
  28.8 144.2 %copy-start.29 = (pred[128,128]{0,1:T(8,128)(4,1)}, pred[128,128]{0,1:T(8,128)(4,1)S(1)}, u32[]{:S(2)}) copy-start(pred[128,128]{0,1:T(8,128)(4,1)S(1)} %iota_compare_fusion.1) | copy-start | bytes 49156
  28.8 109.9 %copy-start.38 = (s32[1024]{0:T(1024)}, s32[1024]{0:T(1024)S(1)}, u32[]{:S(2)}) copy-start(s32[1024]{0:T(1024)S(1)} %pad_clamp_fusion.1) | copy-start | bytes 12292
  28.8 161.8 %copy-start.37 = (s32[1024]{0:T(1024)}, s32[1024]{0:T(1024)S(1)}, u32[]{:S(2)}) copy-start(s32[1024]{0:T(1024)S(1)} %pad_clamp_fusion) | copy-start | bytes 12292
  28.9 145.3 %copy-start.23 = (pred[16,1024]{1,0:T(8,128)(4,1)}, pred[16,1024]{1,0:T(8,128)(4,1)S(1)}, u32[]{:S(2)}) copy-start(pred[16,1024]{1,0:T(8,128)(4,1)S(1)} %iota_compare_fusion.2) | copy-start | bytes 49156
  73.5 58.5 %copy-start.31 = (f32[2048]{0:T(1024)}, f32[2048]{0:T(1024)S(1)}, u32[]{:S(2)}) copy-start(f32[2048]{0:T(1024)S(1)} %get-tuple-element.18) | copy-start | bytes 24580
  126.7 5.8 copy-start.9
  132.0 6.8 copy-start.35
  141.1 1.8 copy-start.12
  141.3 1.5 copy-start.18
  147.8 9.3 copy-start.3
  147.8 4.0 copy-start.13
  157.1 15.8 %copy-start = (f32[1024,16,128,4]{2,0,3,1:T(8,128)}, f32[1024,16,128,4]{2,0,3,1:T(8,128)S(1)}, u32[]{:S(2)}) copy-start(f32[1024,16,128,4]{2,0,3,1:T(8,128)S(1)} %get-tuple-element.37) | copy-start | bytes 100663296
  157.1 17.1 %copy-start.21 = (f32[16,4,128]{2,1,0:T(4,128)}, f32[16,4,128]{2,1,0:T(4,128)S(1)}, u32[]{:S(2)}) copy-start(f32[16,4,128]{2,1,0:T(4,128)S(1)} %max.8) | copy-start | bytes 98308
  163.6 9.3 copy-start.1
  163.7 9.3 copy-start.27
  172.9 1.3 copy-start.25
  173.0 1.3 copy-start.19
  190.0 21.0 %copy-start.7 = (bf16[256,2048]{1,0:T(8,128)(2,1)S(1)}, bf16[256,2048]{1,0:T(8,128)(2,1)}, u32[]{:S(2)}) copy-start(bf16[256,2048]{1,0:T(8,128)(2,1)} %param.13) | copy-start | bytes 3145732
  218.7 2.6 copy-start.10
  219.9 204.7 %all-gather.17.cloned.1.call-start = ((), (), s32[]{:S(2)}) async-start(), calls=%async_computation.16 | async-start | bytes 5242880 | tf_op jit(solution)/shard_map/all_gather | solution.py:38
  220.5 284.6 %all-gather.21.cloned.1.call-start = ((), (), s32[]{:S(2)}) async-start(), calls=%async_computation.18 | async-start | bytes 5242880 | tf_op jit(solution)/shard_map/all_gather | solution.py:38
  221.3 339.3 %all-gather.23.cloned.1.call-start = ((), (), s32[]{:S(2)}) async-start(), calls=%async_computation.20 | async-start | bytes 9437184 | tf_op jit(solution)/shard_map/all_gather | solution.py:38
  222.5 446.6 %reduce-scatter.9.cloned.1.call-start = ((), (), s32[]{:S(2)}) async-start(), calls=%async_computation.19 | async-start | bytes 9437184 | tf_op jit(solution)/shard_map/reduce_scatter | solution.py:42
  597.7 146.5 %reduce-scatter.11.cloned.1.call-start = ((), (), s32[]{:S(2)}) async-start(), calls=%async_computation.21 | async-start | bytes 9437184 | tf_op jit(solution)/shard_map/reduce_scatter | solution.py:42
  597.7 16.5 %copy-start.41 = (bf16[2048,1024]{1,0:T(8,128)(2,1)S(1)}, bf16[2048,1024]{1,0:T(8,128)(2,1)}, u32[]{:S(2)}) copy-start(bf16[2048,1024]{1,0:T(8,128)(2,1)} %all-gather.19.cloned.1.call-done) | copy-start | bytes 12582916
  630.3 337.8 %reduce-scatter.13.cloned.1.call-start = ((), (), s32[]{:S(2)}) async-start(), calls=%async_computation.22 | async-start | bytes 9437184 | tf_op jit(solution)/shard_map/reduce_scatter | solution.py:42
  744.2 4.5 copy-start.11
  749.2 6.5 copy-start.5
  755.7 19.4 %copy-start.22 = (f32[16,4,128]{2,1,0:T(4,128)S(1)}, f32[16,4,128]{2,1,0:T(4,128)}, u32[]{:S(2)}) copy-start(f32[16,4,128]{2,1,0:T(4,128)} %copy-done.21) | copy-start | bytes 98308
  755.7 19.4 %copy-start.26 = (f32[16,4,128]{2,1,0:T(4,128)S(1)}, f32[16,4,128]{2,1,0:T(4,128)}, u32[]{:S(2)}) copy-start(f32[16,4,128]{2,1,0:T(4,128)} %copy-done.25) | copy-start | bytes 98308
  755.7 19.4 %copy-start.30 = (pred[128,128]{0,1:T(8,128)(4,1)S(1)}, pred[128,128]{0,1:T(8,128)(4,1)}, u32[]{:S(2)}) copy-start(pred[128,128]{0,1:T(8,128)(4,1)} %copy-done.29) | copy-start | bytes 49156
  775.2 4.1 copy-start.2
  775.2 4.1 copy-start.28
  779.3 3.3 copy-start.20
  779.3 3.3 copy-start.24
  851.7 5.1 copy-start.4
  856.8 1.9 copy-start.14
  868.8 10.9 copy-start.15
  888.9 8.7 copy-start.16
  897.6 149.6 %reduce-scatter.23.cloned.1.call-start = ((), (), s32[]{:S(2)}) async-start(), calls=%async_computation.27 | async-start | bytes 5242880 | tf_op jit(solution)/shard_map/reduce_scatter | solution.py:42
  912.2 214.6 %reduce-scatter.21.cloned.1.call-start = ((), (), s32[]{:S(2)}) async-start(), calls=%async_computation.26 | async-start | bytes 5242880 | tf_op jit(solution)/shard_map/reduce_scatter | solution.py:42
  926.5 279.8 %reduce-scatter.19.cloned.1.call-start = ((), (), s32[]{:S(2)}) async-start(), calls=%async_computation.25 | async-start | bytes 5242880 | tf_op jit(solution)/shard_map/reduce_scatter | solution.py:42
  941.0 0.7 copy-start.34
  941.0 0.7 copy-start.33
  941.0 1.4 copy-start.17
  941.0 1.4 copy-start.32
  941.0 1.4 copy-start.36
  941.1 311.9 %reduce-scatter.15.cloned.1.call-start = ((), (), s32[]{:S(2)}) async-start(), calls=%async_computation.23 | async-start | bytes 2621440 | tf_op jit(solution)/shard_map/reduce_scatter | solution.py:42
  942.4 25.7 %copy-start.8 = (bf16[256,2048]{1,0:T(8,128)(2,1)S(1)}, bf16[256,2048]{1,0:T(8,128)(2,1)}, u32[]{:S(2)}) copy-start(bf16[256,2048]{1,0:T(8,128)(2,1)} %param.13) | copy-start | bytes 3145732
  951.1 22.2 %copy-start.6 = (f32[256,2048]{1,0:T(8,128)S(1)}, f32[256,2048]{1,0:T(8,128)}, u32[]{:S(2)}) copy-start(f32[256,2048]{1,0:T(8,128)} %copy-done.5) | copy-start | bytes 6291460
  973.1 430.1 %reduce-scatter.17.cloned.1.call-start = ((), (), s32[]{:S(2)}) async-start(), calls=%async_computation.24 | async-start | bytes 8650752 | tf_op jit(solution)/shard_map/reduce_scatter | solution.py:42
  1255.0 150.0 %all-to-all-start.3 = ((bf16[8,64,512]{2,1,0:T(8,128)(2,1)}), bf16[8,64,512]{2,1,0:T(8,128)(2,1)}, u32[]{:S(2)}, u32[]{:S(2)}) async-start(bf16[8,64,512]{2,1,0:T(8,128)(2,1)} %bitcast.303), calls=%async_computation.7 | async-start | bytes 1048576 | tf_op jit(solution)/shard_map/all_to_all | solution.py:220
Sparse Core Ops, SparseCore 0:
  26.3 45.2 all-gather.10
  73.5 53.1 all-gather.8
  129.6 77.4 all-gather.12
  208.5 79.1 all-gather.18
  290.0 52.5 all-gather.14
  344.0 80.5 all-gather.16
  426.2 78.9 all-gather.20
  507.6 52.9 all-gather.22
  597.8 71.2 reduce-scatter.8
  672.8 71.2 reduce-scatter.10
  897.7 70.3 reduce-scatter.12
  970.4 76.7 reduce-scatter.22
  1049.5 77.2 reduce-scatter.20
  1129.0 77.2 reduce-scatter.18
  1208.5 44.4 reduce-scatter.14
  1255.2 147.9 reduce-scatter.16
